TPU v7x, 128 devices: a whole 4x4x4 slice. The times are simulated.
128 devices in a mesh: row: 16 (over z, y_lo, core), pair: 8 (over y_hi, x).
Axes of the slice: x: 4, y: 4 (y_hi: 2, y_lo: 2; y = y_hi * 2 + y_lo), z: 4, core: 2. Of those that a mesh axis runs over, the one named last changes fastest.
Arguments:
- slab: float32 [4096, 4096], P(('row', 'pair'))
- plan: int32 [2, 16], replicated, may hold values from 0 to 15, as said below
Outputs:
- rotated: float32 [4096, 4096], P(('row', 'pair'))
- sing_vals: float32 [4096], replicated
Inputs may be any that keep to these rules, and one draw needn't show every extreme that they name: Each row of plan is a permutation of the block ids; no two blocks form a pair in two rounds, and the two blocks of a pair in round r sit in two different pairs in round r + 1.
All inputs are finite; a program needn't handle non-finite values.
Results may differ from a plain program's by a relative error of at most 0.00017.
Values sent between devices are 32-bit elements; how exact they have to be, the bound alone decides.
A program may use at most 64 MiB of HBM per device.

v0:
```python
import jax
import jax.numpy as jnp
from jax import lax
from jax.sharding import PartitionSpec as P

ROUNDS = 2
NS_STEPS = 4


HIGH = lax.Precision.HIGHEST


def position(order):
    count = order.shape[0]
    slots = jnp.arange(count, dtype=jnp.int32)
    return jnp.sum(jnp.where(order[None, :] == slots[:, None], slots[None, :], 0), axis=1)


def build_turn(cross, diag_vals, width):
    coupling = cross / (diag_vals[:width, None] + diag_vals[None, width:] + 1e-06)
    zero_part = jnp.zeros((width, width), jnp.float32)
    skew = jnp.concatenate(
        [jnp.concatenate([zero_part, coupling], 1), jnp.concatenate([-coupling.T, zero_part], 1)], 0
    )
    scale_c = jnp.sqrt(1.0 + jnp.sum(coupling * coupling))
    ident = jnp.eye(2 * width, dtype=jnp.float32)
    turn = (ident + skew) / scale_c
    for step in range(NS_STEPS):
        inner = jnp.dot(turn.T, turn, precision=HIGH, preferred_element_type=jnp.float32)
        turn = 0.5 * jnp.dot(
            turn, 3.0 * ident - inner, precision=HIGH, preferred_element_type=jnp.float32
        )
    return turn


def on_device(slab, plan):
    piece_rows, ncols = slab.shape
    pair_count = lax.axis_size("pair")
    nblocks = 2 * pair_count
    width = ncols // nblocks
    mine_index = lax.axis_index("pair")
    pieces = slab.reshape(piece_rows, nblocks, width)
    ordered = jnp.take(pieces, plan[0], axis=1)
    local = lax.all_to_all(ordered, "pair", split_axis=1, concat_axis=0, tiled=True)
    group_rows = local.shape[0]
    local = local.reshape(group_rows, 2 * width)
    for rnd in range(ROUNDS):
        if rnd > 0:
            prev_order = plan[rnd - 1]
            next_order = plan[rnd]
            prev_pos = position(prev_order)
            halves = local.reshape(group_rows, 2, width)
            held = lax.dynamic_slice(prev_order, (2 * mine_index,), (2,))
            target = position(next_order)[held] // 2
            owners = jnp.arange(pair_count, dtype=jnp.int32)[:, None, None]
            outgoing = jnp.where(owners == target[0], halves[None, :, 0, :], 0.0) + jnp.where(
                owners == target[1], halves[None, :, 1, :], 0.0
            )
            arrived = lax.all_to_all(outgoing, "pair", split_axis=0, concat_axis=0, tiled=True)
            wanted = lax.dynamic_slice(next_order, (2 * mine_index,), (2,))
            sources = prev_pos[wanted] // 2
            chosen = jnp.take(arrived, sources, axis=0)
            local = jnp.moveaxis(chosen, 0, 1).reshape(group_rows, 2 * width)
        partial_gram = jnp.dot(local.T, local, precision=HIGH, preferred_element_type=jnp.float32)
        gram = lax.psum(partial_gram, "row")
        turn = build_turn(gram[:width, width:], jnp.diagonal(gram), width)
        local = jnp.dot(local, turn, precision=HIGH, preferred_element_type=jnp.float32)
    last_pos = position(plan[ROUNDS - 1])
    back_rows = lax.all_to_all(
        local.reshape(group_rows, 2, width), "pair", split_axis=0, concat_axis=1, tiled=True
    )
    rotated = jnp.take(back_rows, last_pos, axis=1).reshape(piece_rows, ncols)
    squares = lax.psum(jnp.sum(local * local, axis=0), "row")
    scaled = jnp.sqrt(squares / (lax.axis_size("row") * group_rows))
    every = lax.all_gather(scaled, "pair", axis=0, tiled=True)
    sing_vals = jnp.take(every.reshape(nblocks, width), last_pos, axis=0).reshape(ncols)
    return (rotated, sing_vals)


def solution(mesh):
    in_specs = (P(("row", "pair"), None), P())
    out_specs = (P(("row", "pair"), None), P())
    return jax.shard_map(
        on_device, mesh=mesh, in_specs=in_specs, out_specs=out_specs, check_vma=False
    )
```

profile of v0, /device:TPU:0, one launch (start us, length us, event | category | flops | bytes accessed | tf_op | source)
XLA Modules:
  0.0 444.2 jit_solution(5324861720524725574)
XLA Ops:
  7.2 0.0 all-reduce.7.cloned.1.call-start
  7.2 0.8 fusion.24
  8.0 0.1 select_reduce_fusion
  8.1 0.7 compare_and_fusion.1
  8.8 1.1 copy.71
  9.9 0.6 gather_fusion.6
  10.5 0.1 select_bitcast_fusion.1
  10.6 18.4 %all_to_all.38 = f32[32,16,256]{2,0,1:T(8,128)S(1)} all-to-all(f32[32,16,256]{2,0,1:T(8,128)S(1)} %select_bitcast_fusion.1), channel_id=1, replica_groups=mesh['row'=16,'pair'=8] {'pair'}, dimensions={1} | all-to-all | bytes 1048576 | tf_op jit(solution)/shard_map/all_to_all | solution.py:44
  29.0 0.4 copy.42
  29.5 2.1 fusion.26
  31.6 0.0 all-reduce.7.cloned.1.call-update
  31.6 0.1 fusion.6
  31.7 0.6 gather_fusion.1
  32.3 0.6 fusion.25
  32.9 0.6 iota_compare_fusion.5
  33.6 0.7 iota_compare_fusion.6
  34.2 0.4 reshape.265
  34.7 115.9 %all-reduce.7.cloned.1.call-done = f32[512,512]{1,0:T(8,128)} async-done(((f32[512,512]{1,0:T(8,128)}), f32[512,512]{1,0:T(8,128)}) %all-reduce.7.cloned.1.call-update) | async-done | bytes 1048592 | tf_op jit(solution)/shard_map/psum | solution.py:65
  150.5 8.6 %gather_fusion.2 = f32[512]{0:T(512)S(1)} fusion(f32[512,512]{1,0:T(8,128)} %all-reduce.7.cloned.1.call-done, s32[512]{0:T(512)S(1)} %bitcast.103), kind=kCustom, calls=%fused_computation.4 | custom fusion | bytes 8192 | tf_op jit(solution)/shard_map/jit(diagonal)/cond/branch_0_fun/gather | solution.py:66
  159.1 1.7 multiply_reduce_fusion.2
  160.8 0.1 copy.43
  161.7 1.9 select_subtract_fusion.7
  163.6 3.5 convolution_multiply_fusion.7
  167.1 1.9 select_subtract_fusion.6
  169.0 1.9 convolution_multiply_fusion.6
  170.9 1.9 select_subtract_fusion.5
  172.8 2.1 convolution_multiply_fusion.5
  175.0 1.9 select_subtract_fusion.4
  176.9 1.9 convolution_multiply_fusion.4
  178.8 1.1 fusion.27
  179.9 1.6 select_add_fusion
  181.5 6.4 %all-to-all-start.1 = ((f32[8,256,256]{2,1,0:T(8,128)}), f32[8,256,256]{2,1,0:T(8,128)S(1)}, u32[]{:S(2)}, u32[]{:S(2)}) async-start(f32[8,256,256]{2,1,0:T(8,128)} %select_add_fusion), calls=%async_computation.1 | async-start | bytes 4194304 | tf_op jit(solution)/shard_map/all_to_all | solution.py:59
  187.9 0.0 all-reduce.9.cloned.1.call-start
  188.0 0.1 select_reduce_fusion.1
  188.1 0.6 gather_fusion
  188.8 27.2 %all-to-all-done.1 = f32[8,256,256]{2,1,0:T(8,128)S(1)} async-done(((f32[8,256,256]{2,1,0:T(8,128)}), f32[8,256,256]{2,1,0:T(8,128)S(1)}, u32[]{:S(2)}, u32[]{:S(2)}) %all-to-all-start.1) | async-done | bytes 2097184 | tf_op jit(solution)/shard_map/all_to_all | solution.py:59
  216.0 0.6 gather_fusion.3
  216.6 0.1 select_bitcast_fusion.2
  216.7 0.2 copy.48
  216.9 2.1 fusion.28
  219.0 0.0 all-reduce.9.cloned.1.call-update
  219.1 117.3 %all-reduce.9.cloned.1.call-done = f32[512,512]{1,0:T(8,128)} async-done(((f32[512,512]{1,0:T(8,128)}), f32[512,512]{1,0:T(8,128)}) %all-reduce.9.cloned.1.call-update) | async-done | bytes 1048592 | tf_op jit(solution)/shard_map/psum | solution.py:65
  336.4 8.8 %gather_fusion.4 = f32[512]{0:T(512)S(1)} fusion(f32[512,512]{1,0:T(8,128)} %all-reduce.9.cloned.1.call-done, s32[512]{0:T(512)S(1)} %bitcast.104), kind=kCustom, calls=%fused_computation.6 | custom fusion | bytes 8192 | tf_op jit(solution)/shard_map/jit(diagonal)/cond/branch_0_fun/gather | solution.py:66
  345.2 1.7 multiply_reduce_fusion.1
  346.9 0.1 copy.65
  347.8 1.9 select_subtract_fusion.3
  349.7 3.5 convolution_multiply_fusion.3
  353.2 1.9 select_subtract_fusion.2
  355.1 1.9 convolution_multiply_fusion.2
  357.0 1.9 select_subtract_fusion.1
  358.9 2.1 convolution_multiply_fusion.1
  361.0 1.9 select_subtract_fusion
  362.9 1.9 convolution_multiply_fusion
  364.8 1.2 multiply_reduce_fusion
  366.0 1.1 reshape.193
  367.1 6.4 %all-to-all-start.2 = ((f32[256,2,256]{2,1,0:T(2,128)}), f32[256,2,256]{2,1,0:T(2,128)S(1)}, u32[]{:S(2)}, u32[]{:S(2)}) async-start(f32[256,2,256]{2,1,0:T(2,128)} %reshape.193), calls=%async_computation.2 | async-start | bytes 1048576 | tf_op jit(solution)/shard_map/all_to_all | solution.py:69
  373.5 30.2 %psum.23 = f32[512]{0:T(512)S(1)} all-reduce(f32[512]{0:T(512)S(1)} %get-tuple-element.21), channel_id=1, replica_groups=mesh['row'=16,'pair'=8] {'row'}, use_global_device_ids=true, to_apply=%region_7.9 | all-reduce | flops 512 | bytes 4096 | tf_op jit(solution)/shard_map/psum | solution.py:73
  403.7 30.5 %all-gather = f32[8,1,512]{2,1,0:T(1,128)S(1)} all-gather(f32[1,1,512]{2,1,0:T(1,128)S(1)} %bitcast.117), channel_id=1, replica_groups=mesh['row'=16,'pair'=8] {'pair'}, dimensions={0}, use_global_device_ids=true | all-gather | bytes 18432 | tf_op jit(solution)/shard_map/all_gather | solution.py:75
  434.3 0.6 gather_fusion.5
  434.9 0.1 select_bitcast_fusion.3
  434.9 0.6 copy.69
  435.6 0.6 gather_fusion.7
  436.2 0.1 select_bitcast_fusion
  436.3 0.8 copy.67
  (24 shorter events, 0.3 us)
Async XLA Ops:
  7.2 143.4 %all-reduce.7.cloned.1.call-start = ((), (), s32[]{:S(2)}) async-start(), calls=%async_computation.3 | async-start | bytes 2097152 | tf_op jit(solution)/shard_map/psum | solution.py:65
  181.5 34.5 %all-to-all-start.1 = ((f32[8,256,256]{2,1,0:T(8,128)}), f32[8,256,256]{2,1,0:T(8,128)S(1)}, u32[]{:S(2)}, u32[]{:S(2)}) async-start(f32[8,256,256]{2,1,0:T(8,128)} %select_add_fusion), calls=%async_computation.1 | async-start | bytes 4194304 | tf_op jit(solution)/shard_map/all_to_all | solution.py:59
  187.9 148.4 %all-reduce.9.cloned.1.call-start = ((), (), s32[]{:S(2)}) async-start(), calls=%async_computation.4 | async-start | bytes 2097152 | tf_op jit(solution)/shard_map/psum | solution.py:65
  367.1 68.5 %all-to-all-start.2 = ((f32[256,2,256]{2,1,0:T(2,128)}), f32[256,2,256]{2,1,0:T(2,128)S(1)}, u32[]{:S(2)}, u32[]{:S(2)}) async-start(f32[256,2,256]{2,1,0:T(2,128)} %reshape.193), calls=%async_computation.2 | async-start | bytes 1048576 | tf_op jit(solution)/shard_map/all_to_all | solution.py:69
Sparse Core Ops, SparseCore 0:
  31.7 118.7 all-reduce.6
  219.1 117.1 all-reduce.8
where the time goes:
time: 448 us; the launch traced here: 444 us
  waiting for transfers between devices  260 us (58%)
  blocking collectives  79.1 us (18%)
  matrix products  40.4 us (9%)
  local copies, waits for them, and re-layouts  27.5 us (6%)
  between operations  16 us (4%)
  starting transfers between devices  12.9 us (3%)
  other arithmetic  7.91 us (2%)
    psum x2, waiting for transfers between devices, on_device(): gram = lax.psum(partial_gram, 'row')  233 us
    all_gather x1, blocking collectives, on_device(): every = lax.all_gather(scaled, 'pair', axis=0, tiled=True)  30.5 us
    psum x1, blocking collectives, on_device(): squares = lax.psum(jnp.sum(local * local, axis=0), 'row')  30.2 us
    all_to_all x1, waiting for transfers between devices, on_device(): lax.all_to_all(outgoing, 'pair', split_axis=0, concat_axis=0, tiled=True)  27.2 us
    dot_general x8, matrix products, build_turn(): jnp.dot(turn, 3.0 * ident - inner, precision=HIGH, preferred_element_type...  18.6 us
    all_to_all x1, blocking collectives, on_device(): lax.all_to_all(ordered, 'pair', split_axis=1, concat_axis=0, tiled=True)  18.4 us
    gather x2, local copies, waits for them, and re-layouts, on_device(): turn = build_turn(gram[:width, width:], jnp.diagonal(gram), width)  17.4 us
    dot_general x8, matrix products, build_turn(): jnp.dot(turn.T, turn, precision=HIGH, preferred_element_type=jnp.float32)  15.4 us
  transfers between devices with their start and end apart: 4, of which 3 were waited for; matrix products, arithmetic and copies ran while one was open for 1% of the time, Pallas kernels for 0%

commit v1 on v0

v1 whole, which is shorter than its diff:
```python
import functools

import jax
import jax.numpy as jnp
from jax import lax
from jax.experimental import pallas as pl
from jax.experimental.pallas import tpu as pltpu
from jax.sharding import PartitionSpec as P

NS_STEPS = 4
MESH = pl.DeviceIdType.MESH
LANE = 128
ROWS_BY_ROWS = (((1,), (1,)), ((), ()))
PLAIN = (((1,), (0,)), ((), ()))


def split(x):
    high = x.astype(jnp.bfloat16)
    low = (x - high.astype(jnp.float32)).astype(jnp.bfloat16)
    return high, low


def dot3(a, b, dims=PLAIN):
    (ah, al), (bh, bl) = a, b
    mul = functools.partial(
        lax.dot_general, dimension_numbers=dims, preferred_element_type=jnp.float32
    )
    return mul(ah, bh) + (mul(ah, bl) + mul(al, bh))


def column(tile, first, width):
    turned = tile.T
    return jnp.concatenate(
        [turned[:, first + i : first + i + 1] for i in range(width // LANE)], axis=0
    )


def line(tile, first, width):
    return jnp.concatenate(
        [tile[first + i : first + i + 1, :] for i in range(width // LANE)], axis=1
    )


def kernel(
    total_rows,
    plan_ref,
    slab_ref,
    out_ref,
    vals_ref,
    xin,
    send_f,
    recv_f,
    part,
    gather_p,
    dpart,
    gather_d,
    gram,
    send_b,
    recv_b,
    spart,
    gather_s,
    sfin,
    recv_s,
    in_sem,
    f_send,
    f_recv,
    p_send,
    p_recv,
    d_send,
    d_recv,
    g_send,
    g_recv,
    b_send,
    b_recv,
    s_send,
    s_recv,
    v_send,
    v_recv,
):
    nrow, npair = lax.axis_size("row"), lax.axis_size("pair")
    r, p = lax.axis_index("row"), lax.axis_index("pair")
    nblocks = 2 * npair
    rows, width = xin.shape[1:]
    half = width // LANE
    group = npair * rows

    def row_peer(k):
        return lax.rem(r + k, nrow)

    def pair_peer(k):
        return lax.rem(p + k, npair)

    def to_row(src, dst, ssem, rsem, peer):
        return pltpu.make_async_remote_copy(
            src_ref=src, dst_ref=dst, send_sem=ssem, recv_sem=rsem,
            device_id={"row": peer}, device_id_type=MESH,
        )

    def to_pair(src, dst, ssem, rsem, peer):
        return pltpu.make_async_remote_copy(
            src_ref=src, dst_ref=dst, send_sem=ssem, recv_sem=rsem,
            device_id={"pair": peer}, device_id_type=MESH,
        )

    barrier = pltpu.get_barrier_semaphore()
    for k in range(1, nrow):
        pl.semaphore_signal(
            barrier, inc=1, device_id={"row": row_peer(k)}, device_id_type=MESH
        )
    for k in range(1, npair):
        pl.semaphore_signal(
            barrier, inc=1, device_id={"pair": pair_peer(k)}, device_id_type=MESH
        )
    loads = [
        pltpu.make_async_copy(
            slab_ref.at[:, j * width : (j + 1) * width], xin.at[j], in_sem.at[j]
        )
        for j in range(nblocks)
    ]
    for load in loads:
        load.start()

    def locate(block):
        slot = jnp.int32(0)
        for j in range(nblocks):
            slot = jnp.where(plan_ref[1, j] == block, j, slot)
        return slot

    def origin(edge, side):
        keep = plan_ref[1, 2 * edge + side]
        other = jnp.int32(0)
        sign = jnp.float32(0.0)
        for j in range(0, nblocks, 2):
            first, second = plan_ref[0, j], plan_ref[0, j + 1]
            other = jnp.where(first == keep, second, other)
            sign = jnp.where(first == keep, -1.0, sign)
            other = jnp.where(second == keep, first, other)
            sign = jnp.where(second == keep, 1.0, sign)
        return keep, other, sign

    for load in loads:
        load.wait()
    signs = []
    for side in range(2):
        keep, other, sign = origin(p, side)
        signs.append(sign)
        recv_f[side, p, :, :width] = xin[keep]
        recv_f[side, p, :, width:] = xin[other]
        for k in range(1, npair):
            keep, other, _ = origin(pair_peer(k), side)
            send_f[side, k, :, :width] = xin[keep]
            send_f[side, k, :, width:] = xin[other]
    pl.semaphore_wait(barrier, nrow + npair - 2)

    def forward(side, k):
        peer = pair_peer(k)
        return to_pair(
            send_f.at[side, k], recv_f.at[side, p], f_send.at[side, k],
            f_recv.at[side, p], peer,
        )

    def forward_in(side, k):
        peer = pair_peer(k)
        return to_pair(
            send_f.at[side, k], recv_f.at[side, peer], f_send.at[side, k],
            f_recv.at[side, peer], peer,
        )

    for side in range(2):
        for k in range(1, npair):
            forward(side, k).start()

    def reduce_start(n, first, second):
        sums = jnp.concatenate(
            [
                jnp.sum(first * first, axis=0, keepdims=True),
                jnp.sum(second * second, axis=0, keepdims=True),
            ],
            axis=1,
        )
        for i in range(2 * half):
            dpart[n, i : i + 1, :] = sums[:, i * LANE : (i + 1) * LANE]
        gather_d[n, r] = dpart[n]
        for k in range(1, nrow):
            to_row(
                dpart.at[n], gather_d.at[n, r], d_send.at[n, k], d_recv.at[n, r],
                row_peer(k),
            ).start()
        part[n] = dot3(split(first.T), split(second)).reshape(part.shape[1:])
        gather_p[n, r] = part[n, r]
        for k in range(1, nrow):
            peer = row_peer(k)
            to_row(
                part.at[n, peer], gather_p.at[n, r], p_send.at[n, k], p_recv.at[n, r],
                peer,
            ).start()

    def reduce_middle(n):
        for k in range(1, nrow):
            peer = row_peer(k)
            to_row(
                part.at[n, peer], gather_p.at[n, peer], p_send.at[n, k],
                p_recv.at[n, peer], peer,
            ).wait_recv()
        total = gather_p[n, 0]
        for j in range(1, nrow):
            total = total + gather_p[n, j]
        gram[n, r] = total
        for k in range(1, nrow):
            to_row(
                gram.at[n, r], gram.at[n, r], g_send.at[n, k], g_recv.at[n, r],
                row_peer(k),
            ).start()
        for k in range(1, nrow):
            peer = row_peer(k)
            to_row(
                dpart.at[n], gather_d.at[n, peer], d_send.at[n, k], d_recv.at[n, peer],
                peer,
            ).wait_recv()
        sums = gather_d[n, 0]
        for j in range(1, nrow):
            sums = sums + gather_d[n, j]
        return column(sums, 0, width) + (line(sums, half, width) + 1e-6)

    def coupling(n, denom):
        for k in range(1, nrow):
            peer = row_peer(k)
            to_row(
                gram.at[n, r], gram.at[n, peer], g_send.at[n, k], g_recv.at[n, peer],
                peer,
            ).wait_recv()
        return gram[n].reshape(width, width) / denom

    ident = (
        lax.broadcasted_iota(jnp.int32, (width, width), 0)
        == lax.broadcasted_iota(jnp.int32, (width, width), 1)
    ).astype(jnp.float32)

    def rotate(couple, keep, sign_other):
        other, sign = sign_other
        scale = 1.0 + jnp.sum(couple * couple, keepdims=True)
        inv = 1.0 / scale
        pieces = split(couple)
        inner = (ident + dot3(pieces, pieces, ROWS_BY_ROWS)) * inv
        out = (keep + sign * dot3(split(other), pieces, ROWS_BY_ROWS)) * jnp.sqrt(inv)
        for step in range(NS_STEPS):
            factor = 1.5 * ident - 0.5 * inner
            fs = split(factor)
            out = dot3(split(out), fs)
            if step + 1 < NS_STEPS:
                inner = dot3(split(inner), split(dot3(fs, fs)))
        return out

    for side in range(2):
        for k in range(1, npair):
            forward_in(side, k).wait_recv()
        both = recv_f[side].reshape(group, 2 * width)
        reduce_start(side, both[:, :width], both[:, width:])
    denoms = [reduce_middle(side) for side in range(2)]
    blocks = []
    for side in range(2):
        couple = coupling(side, denoms[side])
        both = recv_f[side].reshape(group, 2 * width)
        blocks.append(rotate(couple, both[:, :width], (both[:, width:], signs[side])))

    reduce_start(2, blocks[0], blocks[1])
    couple = coupling(2, reduce_middle(2))
    finals = [
        rotate(couple, blocks[0], (blocks[1], -1.0)),
        rotate(couple.T, blocks[1], (blocks[0], 1.0)),
    ]
    for side in range(2):
        send_b[:, side] = finals[side].reshape(npair, rows, width)
        sums = jnp.sum(finals[side] * finals[side], axis=0, keepdims=True)
        for i in range(half):
            spart[side * half + i : side * half + i + 1, :] = sums[
                :, i * LANE : (i + 1) * LANE
            ]
    gather_s[r] = spart[...]
    for k in range(1, nrow):
        to_row(
            spart, gather_s.at[r], s_send.at[k], s_recv.at[r], row_peer(k)
        ).start()
    mine = pl.ds(2 * p, 2)
    for k in range(1, npair):
        peer = pair_peer(k)
        to_pair(
            send_b.at[peer], recv_b.at[mine], b_send.at[k], b_recv.at[p], peer
        ).start()
    recv_b[mine] = send_b[p]

    for k in range(1, nrow):
        peer = row_peer(k)
        to_row(
            spart, gather_s.at[peer], s_send.at[k], s_recv.at[peer], peer
        ).wait_recv()
    sums = gather_s[0]
    for j in range(1, nrow):
        sums = sums + gather_s[j]
    vals = jnp.sqrt(sums / total_rows)
    for side in range(2):
        sfin[side, :half, :] = vals[side * half : (side + 1) * half]
    for k in range(1, npair):
        to_pair(
            sfin, recv_s.at[mine], v_send.at[k], v_recv.at[p], pair_peer(k)
        ).start()
    recv_s[mine] = sfin[...]

    for k in range(1, npair):
        peer = pair_peer(k)
        to_pair(
            send_b.at[peer], recv_b.at[pl.ds(2 * peer, 2)], b_send.at[k],
            b_recv.at[peer], peer,
        ).wait_recv()
        to_pair(
            sfin, recv_s.at[pl.ds(2 * peer, 2)], v_send.at[k], v_recv.at[peer], peer
        ).wait_recv()
    for j in range(nblocks):
        slot = locate(j)
        out_ref[:, j * width : (j + 1) * width] = recv_b[slot]
        vals_ref[j * half : (j + 1) * half, :] = recv_s[slot, :half, :]

    for side in range(2):
        for k in range(1, npair):
            forward(side, k).wait_send()
    for n in range(3):
        for k in range(1, nrow):
            peer = row_peer(k)
            to_row(
                dpart.at[n], gather_d.at[n, r], d_send.at[n, k], d_recv.at[n, r], peer
            ).wait_send()
            to_row(
                part.at[n, peer], gather_p.at[n, r], p_send.at[n, k], p_recv.at[n, r],
                peer,
            ).wait_send()
            to_row(
                gram.at[n, r], gram.at[n, r], g_send.at[n, k], g_recv.at[n, r], peer
            ).wait_send()
    for k in range(1, nrow):
        to_row(
            spart, gather_s.at[r], s_send.at[k], s_recv.at[r], row_peer(k)
        ).wait_send()
    for k in range(1, npair):
        peer = pair_peer(k)
        to_pair(
            send_b.at[peer], recv_b.at[mine], b_send.at[k], b_recv.at[p], peer
        ).wait_send()
        to_pair(
            sfin, recv_s.at[mine], v_send.at[k], v_recv.at[p], peer
        ).wait_send()


def solution(mesh):
    nrow, npair = mesh.shape["row"], mesh.shape["pair"]

    def on_device(slab, plan):
        rows, ncols = slab.shape
        nblocks = 2 * npair
        width = ncols // nblocks
        part_rows = width // nrow
        half = width // LANE
        f32 = jnp.float32
        dma = pltpu.SemaphoreType.DMA
        out, vals = pl.pallas_call(
            functools.partial(kernel, rows * nrow * npair),
            out_shape=(
                jax.ShapeDtypeStruct((rows, ncols), f32),
                jax.ShapeDtypeStruct((nblocks * half, LANE), f32),
            ),
            in_specs=[
                pl.BlockSpec(memory_space=pltpu.SMEM),
                pl.BlockSpec(memory_space=pl.ANY),
            ],
            out_specs=(
                pl.BlockSpec(memory_space=pltpu.VMEM),
                pl.BlockSpec(memory_space=pltpu.VMEM),
            ),
            scratch_shapes=[
                pltpu.VMEM((nblocks, rows, width), f32),
                pltpu.VMEM((2, npair, rows, 2 * width), f32),
                pltpu.VMEM((2, npair, rows, 2 * width), f32),
                pltpu.VMEM((3, nrow, part_rows, width), f32),
                pltpu.VMEM((3, nrow, part_rows, width), f32),
                pltpu.VMEM((3, 8, LANE), f32),
                pltpu.VMEM((3, nrow, 8, LANE), f32),
                pltpu.VMEM((3, nrow, part_rows, width), f32),
                pltpu.VMEM((npair, 2, rows, width), f32),
                pltpu.VMEM((nblocks, rows, width), f32),
                pltpu.VMEM((8, LANE), f32),
                pltpu.VMEM((nrow, 8, LANE), f32),
                pltpu.VMEM((2, 8, LANE), f32),
                pltpu.VMEM((nblocks, 8, LANE), f32),
                dma((nblocks,)),
                dma((2, npair)),
                dma((2, npair)),
                dma((3, nrow)),
                dma((3, nrow)),
                dma((3, nrow)),
                dma((3, nrow)),
                dma((3, nrow)),
                dma((3, nrow)),
                dma((npair,)),
                dma((npair,)),
                dma((nrow,)),
                dma((nrow,)),
                dma((npair,)),
                dma((npair,)),
            ],
            compiler_params=pltpu.CompilerParams(
                collective_id=0, has_side_effects=True, vmem_limit_bytes=48 * 2**20
            ),
        )(plan, slab)
        return out, vals.reshape(ncols)

    return jax.shard_map(
        on_device,
        mesh=mesh,
        in_specs=(P(("row", "pair"), None), P()),
        out_specs=(P(("row", "pair"), None), P()),
        check_vma=False,
    )
```

time: 448 us -> 75 us (0.17)
  waiting for transfers between devices: 260 us -> 0 us
  blocking collectives: 79.1 us -> 0 us
  Pallas kernels: 0 us -> 70.9 us
  matrix products: 40.4 us -> 0 us
  local copies, waits for them, and re-layouts: 27.5 us -> 3.12 us
  between operations: 16 us -> 0.65 us
  starting transfers between devices: 12.9 us -> 0 us
  other arithmetic: 7.91 us -> 0 us
    psum x2 -> x0, waiting for transfers between devices: 233 us -> none  [on_device(): gram = lax.psum(partial_gram, 'row')]
    pallas_call x0 -> x1, Pallas kernels: none -> 70.9 us  [on_device(): pl.pallas_call(functools.partial(kernel, rows * nrow * npair), out_shape=...]
    dot_general x20 -> x0, matrix products: 40.4 us -> none  [the longest x8 18.6 us: build_turn(): jnp.dot(turn, 3.0 * ident - inner, precision=HIGH, preferred_element_type...]
    all_gather x1 -> x0, blocking collectives: 30.5 us -> none  [on_device(): every = lax.all_gather(scaled, 'pair', axis=0, tiled=True)]
    psum x1 -> x0, blocking collectives: 30.2 us -> none  [on_device(): squares = lax.psum(jnp.sum(local * local, axis=0), 'row')]
    all_to_all x2 -> x0, waiting for transfers between devices: 27.2 us -> none  [the longest x1 27.2 us: on_device(): lax.all_to_all(outgoing, 'pair', split_axis=0, concat_axis=0, tiled=True)]
    gather x8 -> x0, local copies, waits for them, and re-layouts: 21 us -> none  [the longest x2 17.4 us: on_device(): turn = build_turn(gram[:width, width:], jnp.diagonal(gram), width)]
    all_to_all x1 -> x0, blocking collectives: 18.4 us -> none  [on_device(): lax.all_to_all(ordered, 'pair', split_axis=1, concat_axis=0, tiled=True)]
  transfers between devices with their start and end apart: 4 -> 0, of which waited for: 3 -> 0; matrix products, arithmetic and copies ran while one was open for 1% -> 0% of each run, Pallas kernels for 0% -> 0%
where the time goes in v1:
time: 75 us; the launch traced here: 74.7 us
  Pallas kernels  70.9 us (95%)
  local copies, waits for them, and re-layouts  3.12 us (4%)
    pallas_call x1, Pallas kernels, on_device(): pl.pallas_call(functools.partial(kernel, rows * nrow * npair), out_shape=...  70.9 us
    unnamed x6, local copies, waits for them, and re-layouts  3.12 us

profile of v1, /device:TPU:0, one launch (start us, length us, event | category | flops | bytes accessed | tf_op | source)
XLA Modules:
  0.0 74.7 jit_solution(15693470308092267508)
XLA Ops:
  0.6 0.0 copy-start
  0.6 1.0 %copy-done = f32[32,4096]{1,0:T(8,128)S(1)} copy-done((f32[32,4096]{1,0:T(8,128)S(1)}, f32[32,4096]{1,0:T(8,128)}, u32[]{:S(2)}) %copy-start) | copy-done | bytes 524312
  1.7 0.0 copy-start.1
  1.7 0.7 copy-done.1
  2.4 70.9 %shard_map.41 = (f32[32,4096]{1,0:T(8,128)S(1)}, f32[32,128]{1,0:T(8,128)S(1)}) custom-call(s32[2,16]{1,0:T(2,128)S(1)} %copy-done.1, f32[32,4096]{1,0:T(8,128)S(1)} %copy-done), custom_call_target="tpu_custom_call" | custom-call | tf_op jit(solution)/shard_map/pallas_call | solution.py:364
  73.3 0.8 %copy.6 = f32[32,4096]{1,0:T(8,128)} copy(f32[32,4096]{1,0:T(8,128)S(1)} %get-tuple-element.8) | data formatting | bytes 1048576
  74.1 0.6 copy.7
Async XLA Ops:
  0.6 1.0 %copy-start = (f32[32,4096]{1,0:T(8,128)S(1)}, f32[32,4096]{1,0:T(8,128)}, u32[]{:S(2)}) copy-start(f32[32,4096]{1,0:T(8,128)} %slab_ref.1) | copy-start | bytes 1572868
  1.7 0.7 copy-start.1

commit v2 on v1

v2 whole, which is shorter than its diff:
```python
import functools

import jax
import jax.numpy as jnp
from jax import lax
from jax.experimental import pallas as pl
from jax.experimental.pallas import tpu as pltpu
from jax.sharding import PartitionSpec as P

NS_STEPS = 4
MESH = pl.DeviceIdType.MESH
LANE = 128
ROWS_BY_ROWS = (((1,), (1,)), ((), ()))
PLAIN = (((1,), (0,)), ((), ()))


def split(x):
    high = x.astype(jnp.bfloat16)
    low = (x - high.astype(jnp.float32)).astype(jnp.bfloat16)
    return high, low


def dot3(a, b, dims=PLAIN):
    (ah, al), (bh, bl) = a, b
    mul = functools.partial(
        lax.dot_general, dimension_numbers=dims, preferred_element_type=jnp.float32
    )
    return mul(ah, bh) + (mul(ah, bl) + mul(al, bh))


def column(tile, first, width):
    turned = tile.T
    return jnp.concatenate(
        [turned[:, first + i : first + i + 1] for i in range(width // LANE)], axis=0
    )


def line(tile, first, width):
    return jnp.concatenate(
        [tile[first + i : first + i + 1, :] for i in range(width // LANE)], axis=1
    )


def ring_places(r, p, nrow, npair):
    def slot_peer(slot):
        return {"row": r, "pair": slot}

    def rank_peer(rank):
        return {"row": rank, "pair": p}

    return p, r, slot_peer, rank_peer


def torus_places(r, p):
    core, y_lo, z = lax.rem(r, 2), lax.rem(lax.div(r, 2), 2), lax.div(r, 4)
    y_hi, x = lax.div(p, 4), lax.rem(p, 4)
    y = 2 * y_hi + y_lo

    def device(x, y, z, core):
        return {
            "row": (z * 2 + lax.rem(y, 2)) * 2 + core,
            "pair": lax.div(y, 2) * 4 + x,
        }

    turn = lax.rem(x + z + 2 * y_hi, 4)
    y_other = lax.div(lax.rem(y + 3, 4), 2)

    def slot_peer(slot):
        i, b = lax.div(slot, 2), lax.rem(slot, 2)
        x0 = lax.rem(i - z - 2 * y_hi + 8, 4)
        y1 = lax.rem(2 * y_other + 2 - b, 4)
        z1 = lax.rem(i - x - 2 * lax.div(y1, 2) + 8, 4)
        first = core == 0
        return device(
            jnp.where(first, x0, x),
            jnp.where(first, 2 * y_hi + b, y1),
            jnp.where(first, z, z1),
            core,
        )

    def rank_peer(rank):
        far, t = lax.div(rank, 8), lax.rem(lax.div(rank, 2), 4)
        return device(
            t, y_lo + 2 * far, lax.rem(turn - t - 2 * far + 8, 4), lax.rem(rank, 2)
        )

    return 2 * turn + y_lo, (y_hi * 4 + x) * 2 + core, slot_peer, rank_peer


def locate(plan_ref, block, nblocks):
    slot = jnp.int32(0)
    for j in range(nblocks):
        slot = jnp.where(plan_ref[1, j] == block, j, slot)
    return slot


def kernel(
    total_rows,
    plan_hbm,
    slab_ref,
    recv_b,
    recv_s,
    plan_ref,
    xin,
    send_f,
    recv_f,
    part,
    gather_p,
    dpart,
    gather_d,
    gram,
    send_b,
    spart,
    gather_s,
    sfin,
    in_sem,
    f_send,
    f_recv,
    p_send,
    p_recv,
    d_send,
    d_recv,
    g_send,
    g_recv,
    b_send,
    b_recv,
    s_send,
    s_recv,
    v_send,
    v_recv,
):
    nrow, npair = lax.axis_size("row"), lax.axis_size("pair")
    row, pair = lax.axis_index("row"), lax.axis_index("pair")
    nblocks = 2 * npair
    rows, width = xin.shape[1:]
    half = width // LANE
    group = npair * rows
    if (nrow, npair) == (16, 8):
        p, r, slot_peer, rank_peer = torus_places(row, pair)
    else:
        p, r, slot_peer, rank_peer = ring_places(row, pair, nrow, npair)
    slots = [lax.rem(p + k, npair) for k in range(npair)]
    ranks = [lax.rem(r + k, nrow) for k in range(nrow)]
    by_slot = [None] + [slot_peer(slot) for slot in slots[1:]]
    by_rank = [None] + [rank_peer(rank) for rank in ranks[1:]]
    others, peers = pl.ds(0, nrow - 1), pl.ds(0, npair - 1)

    def copy_to(device, src, dst, ssem, rsem):
        return pltpu.make_async_remote_copy(
            src_ref=src, dst_ref=dst, send_sem=ssem, recv_sem=rsem,
            device_id=device, device_id_type=MESH,
        )

    barrier = pltpu.get_barrier_semaphore()
    for device in by_slot[1:] + by_rank[1:]:
        pl.semaphore_signal(barrier, inc=1, device_id=device, device_id_type=MESH)
    plan_load = pltpu.make_async_copy(plan_hbm, plan_ref, in_sem.at[0])
    plan_load.start()
    for j in range(nblocks):
        pltpu.make_async_copy(
            slab_ref.at[:, j * width : (j + 1) * width], xin.at[j], in_sem.at[1]
        ).start()
    plan_load.wait()

    def origin(edge, side):
        keep = plan_ref[1, 2 * edge + side]
        other = jnp.int32(0)
        sign = jnp.float32(0.0)
        for j in range(0, nblocks, 2):
            first, second = plan_ref[0, j], plan_ref[0, j + 1]
            other = jnp.where(first == keep, second, other)
            sign = jnp.where(first == keep, -1.0, sign)
            other = jnp.where(second == keep, first, other)
            sign = jnp.where(second == keep, 1.0, sign)
        return keep, other, sign

    pltpu.make_async_copy(xin, xin, in_sem.at[1]).wait()
    signs = []
    for side in range(2):
        keep, other, sign = origin(p, side)
        signs.append(sign)
        recv_f[side, p, :, :width] = xin[keep]
        recv_f[side, p, :, width:] = xin[other]
        for k in range(1, npair):
            keep, other, _ = origin(slots[k], side)
            send_f[side, k - 1, :, :width] = xin[keep]
            send_f[side, k - 1, :, width:] = xin[other]
    pl.semaphore_wait(barrier, nrow + npair - 2)

    for side in range(2):
        for k in range(1, npair):
            copy_to(
                by_slot[k], send_f.at[side, k - 1], recv_f.at[side, p], f_send,
                f_recv.at[side],
            ).start()

    def wait_recv(ref, sem):
        copy_to(by_rank[1], ref, ref, sem, sem).wait_recv()

    def wait_send(ref, sem):
        copy_to(by_rank[1], ref, ref, sem, sem).wait_send()

    def reduce_start(n, first, second):
        sums = jnp.concatenate(
            [
                jnp.sum(first * first, axis=0, keepdims=True),
                jnp.sum(second * second, axis=0, keepdims=True),
            ],
            axis=1,
        )
        for i in range(2 * half):
            dpart[n, i : i + 1, :] = sums[:, i * LANE : (i + 1) * LANE]
        gather_d[n, r] = dpart[n]
        for k in range(1, nrow):
            copy_to(
                by_rank[k], dpart.at[n], gather_d.at[n, r], d_send, d_recv.at[n]
            ).start()
        part[n] = dot3(split(first.T), split(second)).reshape(part.shape[1:])
        gather_p[n, r] = part[n, r]
        for k in range(1, nrow):
            copy_to(
                by_rank[k], part.at[n, ranks[k]], gather_p.at[n, r], p_send,
                p_recv.at[n],
            ).start()

    def reduce_middle(n):
        wait_recv(gather_p.at[n, others], p_recv.at[n])
        total = gather_p[n, 0]
        for j in range(1, nrow):
            total = total + gather_p[n, j]
        gram[n, r] = total
        for k in range(1, nrow):
            copy_to(
                by_rank[k], gram.at[n, r], gram.at[n, r], g_send, g_recv.at[n]
            ).start()
        wait_recv(gather_d.at[n, others], d_recv.at[n])
        sums = gather_d[n, 0]
        for j in range(1, nrow):
            sums = sums + gather_d[n, j]
        return column(sums, 0, width) + (line(sums, half, width) + 1e-6)

    def coupling(n, denom):
        wait_recv(gram.at[n, others], g_recv.at[n])
        return gram[n].reshape(width, width) / denom

    ident = (
        lax.broadcasted_iota(jnp.int32, (width, width), 0)
        == lax.broadcasted_iota(jnp.int32, (width, width), 1)
    ).astype(jnp.float32)

    def rotate(couple, keep, sign_other):
        other, sign = sign_other
        scale = 1.0 + jnp.sum(couple * couple, keepdims=True)
        inv = 1.0 / scale
        pieces = split(couple)
        inner = (ident + dot3(pieces, pieces, ROWS_BY_ROWS)) * inv
        out = (keep + sign * dot3(split(other), pieces, ROWS_BY_ROWS)) * jnp.sqrt(inv)
        for step in range(NS_STEPS):
            factor = 1.5 * ident - 0.5 * inner
            fs = split(factor)
            out = dot3(split(out), fs)
            if step + 1 < NS_STEPS:
                inner = dot3(split(inner), split(dot3(fs, fs)))
        return out

    for side in range(2):
        wait_recv(recv_f.at[side, peers], f_recv.at[side])
        both = recv_f[side].reshape(group, 2 * width)
        reduce_start(side, both[:, :width], both[:, width:])
    denoms = [reduce_middle(side) for side in range(2)]
    blocks = []
    for side in range(2):
        couple = coupling(side, denoms[side])
        both = recv_f[side].reshape(group, 2 * width)
        blocks.append(rotate(couple, both[:, :width], (both[:, width:], signs[side])))

    reduce_start(2, blocks[0], blocks[1])
    couple = coupling(2, reduce_middle(2))
    finals = [
        rotate(couple, blocks[0], (blocks[1], -1.0)),
        rotate(couple.T, blocks[1], (blocks[0], 1.0)),
    ]
    for side in range(2):
        send_b[:, side] = finals[side].reshape(npair, rows, width)
        sums = jnp.sum(finals[side] * finals[side], axis=0, keepdims=True)
        for i in range(half):
            spart[side * half + i : side * half + i + 1, :] = sums[
                :, i * LANE : (i + 1) * LANE
            ]
    gather_s[r] = spart[...]
    for k in range(1, nrow):
        copy_to(by_rank[k], spart, gather_s.at[r], s_send, s_recv).start()
    mine = pl.ds(2 * p, 2)
    own = pltpu.make_async_copy(send_b.at[p], recv_b.at[mine], in_sem.at[0])
    own.start()
    for k in range(1, npair):
        copy_to(
            by_slot[k], send_b.at[slots[k]], recv_b.at[mine], b_send, b_recv
        ).start()

    wait_recv(gather_s.at[others], s_recv)
    sums = gather_s[0]
    for j in range(1, nrow):
        sums = sums + gather_s[j]
    vals = jnp.sqrt(sums / total_rows)
    for side in range(2):
        sfin[side] = vals[side * half : (side + 1) * half]
    for k in range(1, npair):
        copy_to(by_slot[k], sfin, recv_s.at[mine], v_send, v_recv).start()
    recv_s[mine] = sfin[...]

    own.wait()
    arrived = pl.ds(0, 2 * (npair - 1))
    wait_send(send_f.at[:, peers], f_send)
    wait_send(gather_d.at[:, others], d_send)
    wait_send(gather_p.at[:, others], p_send)
    wait_send(gram.at[:, others], g_send)
    wait_send(gather_s.at[others], s_send)
    wait_send(send_b.at[peers], b_send)
    wait_send(recv_s.at[arrived], v_send)
    wait_recv(recv_b.at[arrived], b_recv)
    wait_recv(recv_s.at[arrived], v_recv)


def place(plan_ref, blocks_ref, vals_in, out_ref, vals_ref, buffer, in_sem, out_sem):
    nblocks, rows, width = blocks_ref.shape
    half = width // LANE
    batch = 4
    slots = [locate(plan_ref, j, nblocks) for j in range(nblocks)]
    loads, stores = [], []
    for j in range(nblocks):
        columns = pl.ds(j * width, width)
        loads.append(
            pltpu.make_async_copy(
                blocks_ref.at[slots[j]], buffer.at[:, columns], in_sem.at[j]
            )
        )
        loads[-1].start()
    for j in range(nblocks):
        vals_ref[j * half : (j + 1) * half, :] = vals_in[slots[j]]
    for j in range(0, nblocks, batch):
        columns = pl.ds(j * width, batch * width)
        for load in loads[j : j + batch]:
            load.wait()
        stores.append(
            pltpu.make_async_copy(
                buffer.at[:, columns], out_ref.at[:, columns], out_sem.at[j // batch]
            )
        )
        stores[-1].start()
    for store in stores:
        store.wait()


def solution(mesh):
    nrow, npair = mesh.shape["row"], mesh.shape["pair"]
    vmem, smem = pltpu.VMEM, pltpu.SMEM
    anywhere = pl.BlockSpec(memory_space=pl.ANY)

    def on_device(slab, plan):
        rows, ncols = slab.shape
        nblocks = 2 * npair
        width = ncols // nblocks
        part_rows = width // nrow
        half = width // LANE
        f32 = jnp.float32
        dma = pltpu.SemaphoreType.DMA
        arrived, arrived_vals = pl.pallas_call(
            functools.partial(kernel, rows * nrow * npair),
            out_shape=(
                jax.ShapeDtypeStruct((nblocks, rows, width), f32),
                jax.ShapeDtypeStruct((nblocks, half, LANE), f32),
            ),
            in_specs=[anywhere, anywhere],
            out_specs=(anywhere, pl.BlockSpec(memory_space=vmem)),
            scratch_shapes=[
                smem(plan.shape, jnp.int32),
                vmem((nblocks, rows, width), f32),
                vmem((2, npair - 1, rows, 2 * width), f32),
                vmem((2, npair, rows, 2 * width), f32),
                vmem((3, nrow, part_rows, width), f32),
                vmem((3, nrow, part_rows, width), f32),
                vmem((3, 2 * half, LANE), f32),
                vmem((3, nrow, 2 * half, LANE), f32),
                vmem((3, nrow, part_rows, width), f32),
                vmem((npair, 2, rows, width), f32),
                vmem((2 * half, LANE), f32),
                vmem((nrow, 2 * half, LANE), f32),
                vmem((2, half, LANE), f32),
                dma((2,)),
                dma,
                dma((2,)),
                dma,
                dma((3,)),
                dma,
                dma((3,)),
                dma,
                dma((3,)),
                dma,
                dma,
                dma,
                dma,
                dma,
                dma,
            ],
            compiler_params=pltpu.CompilerParams(
                collective_id=0, has_side_effects=True, vmem_limit_bytes=67043328
            ),
        )(plan, slab)
        out, vals = pl.pallas_call(
            place,
            out_shape=(
                jax.ShapeDtypeStruct((rows, ncols), f32),
                jax.ShapeDtypeStruct((nblocks * half, LANE), f32),
            ),
            in_specs=[
                pl.BlockSpec(memory_space=smem),
                anywhere,
                pl.BlockSpec(memory_space=vmem),
            ],
            out_specs=(anywhere, pl.BlockSpec(memory_space=vmem)),
            scratch_shapes=[vmem((rows, ncols), f32), dma((nblocks,)), dma((4,))],
            compiler_params=pltpu.CompilerParams(vmem_limit_bytes=67043328),
        )(plan, arrived, arrived_vals)
        return out, vals.reshape(ncols)

    return jax.shard_map(
        on_device,
        mesh=mesh,
        in_specs=(P(("row", "pair"), None), P()),
        out_specs=(P(("row", "pair"), None), P()),
        check_vma=False,
    )
```

time: 75 us -> 71.5 us (0.953)
  local copies, waits for them, and re-layouts: 3.12 us -> 0 us
    pallas_call x1, Pallas kernels: 70.9 us -> 67.1 us  [on_device(): pl.pallas_call(functools.partial(kernel, rows * nrow * npair), out_shape=...]
    pallas_call x0 -> x1, Pallas kernels: none -> 3.21 us  [on_device(): pl.pallas_call(place, out_shape=(jax.ShapeDtypeStruct((rows, ncols), f32)...]
    unnamed x6 -> x0, local copies, waits for them, and re-layouts: 3.12 us -> none
where the time goes in v2:
time: 71.5 us; the launch traced here: 70.9 us
  Pallas kernels  70.3 us (98%)
    pallas_call x1, Pallas kernels, on_device(): pl.pallas_call(functools.partial(kernel, rows * nrow * npair), out_shape=...  67.1 us
    pallas_call x1, Pallas kernels, on_device(): pl.pallas_call(place, out_shape=(jax.ShapeDtypeStruct((rows, ncols), f32)...  3.21 us

profile of v2, /device:TPU:0, one launch (start us, length us, event | category | flops | bytes accessed | tf_op | source)
XLA Modules:
  0.0 70.9 jit_solution(1657704268434852493)
XLA Ops:
  0.6 67.1 %shard_map.41 = (f32[16,32,256]{2,1,0:T(8,128)}, f32[16,2,128]{2,1,0:T(2,128)}) custom-call(s32[2,16]{1,0:T(2,128)} %plan_ref.1, f32[32,4096]{1,0:T(8,128)} %slab_ref.1), custom_call_target="tpu_custom_call" | custom-call | tf_op jit(solution)/shard_map/pallas_call | solution.py:368
  67.7 3.2 %shard_map.42 = (f32[32,4096]{1,0:T(8,128)}, f32[32,128]{1,0:T(8,128)}) custom-call(s32[2,16]{1,0:T(2,128)} %plan_ref.1, f32[16,32,256]{2,1,0:T(8,128)} %get-tuple-element.6.blocks_ref, f32[16,2,128]{2,1,0:T(2,128)} %get-tuple-element.7.vals_in), custom_call_target="tpu_custom_call" | custom-call | tf_op jit(solution)/shard_map/pallas_call | solution.py:410

commit v3 on v2

--- a/solution.py
+++ b/solution.py
@@ -8,6 +8,7 @@
 from jax.sharding import PartitionSpec as P
 
 NS_STEPS = 4
+CHUNKS = 2
 MESH = pl.DeviceIdType.MESH
 LANE = 128
 ROWS_BY_ROWS = (((1,), (1,)), ((), ()))
@@ -98,6 +99,8 @@
     total_rows,
     plan_hbm,
     slab_ref,
+    out_ref,
+    vals_ref,
     recv_b,
     recv_s,
     plan_ref,
@@ -151,11 +154,11 @@
             device_id=device, device_id_type=MESH,
         )
 
+    plan_load = pltpu.make_async_copy(plan_hbm, plan_ref, in_sem.at[0])
+    plan_load.start()
     barrier = pltpu.get_barrier_semaphore()
     for device in by_slot[1:] + by_rank[1:]:
         pl.semaphore_signal(barrier, inc=1, device_id=device, device_id_type=MESH)
-    plan_load = pltpu.make_async_copy(plan_hbm, plan_ref, in_sem.at[0])
-    plan_load.start()
     for j in range(nblocks):
         pltpu.make_async_copy(
             slab_ref.at[:, j * width : (j + 1) * width], xin.at[j], in_sem.at[1]
@@ -177,22 +180,22 @@
     pltpu.make_async_copy(xin, xin, in_sem.at[1]).wait()
     signs = []
     for side in range(2):
-        keep, other, sign = origin(p, side)
-        signs.append(sign)
-        recv_f[side, p, :, :width] = xin[keep]
-        recv_f[side, p, :, width:] = xin[other]
         for k in range(1, npair):
             keep, other, _ = origin(slots[k], side)
             send_f[side, k - 1, :, :width] = xin[keep]
             send_f[side, k - 1, :, width:] = xin[other]
-    pl.semaphore_wait(barrier, nrow + npair - 2)
-
-    for side in range(2):
+        if side == 0:
+            pl.semaphore_wait(barrier, nrow + npair - 2)
         for k in range(1, npair):
             copy_to(
                 by_slot[k], send_f.at[side, k - 1], recv_f.at[side, p], f_send,
                 f_recv.at[side],
             ).start()
+    for side in range(2):
+        keep, other, sign = origin(p, side)
+        signs.append(sign)
+        recv_f[side, p, :, :width] = xin[keep]
+        recv_f[side, p, :, width:] = xin[other]
 
     def wait_recv(ref, sem):
         copy_to(by_rank[1], ref, ref, sem, sem).wait_recv()
@@ -201,6 +204,15 @@
         copy_to(by_rank[1], ref, ref, sem, sem).wait_send()
 
     def reduce_start(n, first, second):
+        part[n] = dot3(split(first.T), split(second)).reshape(part.shape[1:])
+        for h in range(CHUNKS):
+            for k in range(1, nrow):
+                copy_to(
+                    by_rank[k], part.at[n, h, ranks[k]], gather_p.at[n, h, r], p_send,
+                    p_recv.at[n, h],
+                ).start()
+        for h in range(CHUNKS):
+            gather_p[n, h, r] = part[n, h, r]
         sums = jnp.concatenate(
             [
                 jnp.sum(first * first, axis=0, keepdims=True),
@@ -210,29 +222,23 @@
         )
         for i in range(2 * half):
             dpart[n, i : i + 1, :] = sums[:, i * LANE : (i + 1) * LANE]
-        gather_d[n, r] = dpart[n]
         for k in range(1, nrow):
             copy_to(
                 by_rank[k], dpart.at[n], gather_d.at[n, r], d_send, d_recv.at[n]
             ).start()
-        part[n] = dot3(split(first.T), split(second)).reshape(part.shape[1:])
-        gather_p[n, r] = part[n, r]
-        for k in range(1, nrow):
-            copy_to(
-                by_rank[k], part.at[n, ranks[k]], gather_p.at[n, r], p_send,
-                p_recv.at[n],
-            ).start()
+        gather_d[n, r] = dpart[n]
 
     def reduce_middle(n):
-        wait_recv(gather_p.at[n, others], p_recv.at[n])
-        total = gather_p[n, 0]
-        for j in range(1, nrow):
-            total = total + gather_p[n, j]
-        gram[n, r] = total
-        for k in range(1, nrow):
-            copy_to(
-                by_rank[k], gram.at[n, r], gram.at[n, r], g_send, g_recv.at[n]
-            ).start()
+        for h in range(CHUNKS):
+            wait_recv(gather_p.at[n, h, others], p_recv.at[n, h])
+            total = gather_p[n, h, 0]
+            for j in range(1, nrow):
+                total = total + gather_p[n, h, j]
+            gram[n, h, r] = total
+            for k in range(1, nrow):
+                copy_to(
+                    by_rank[k], gram.at[n, h, r], gram.at[n, h, r], g_send, g_recv.at[n]
+                ).start()
         wait_recv(gather_d.at[n, others], d_recv.at[n])
         sums = gather_d[n, 0]
         for j in range(1, nrow):
@@ -240,7 +246,7 @@
         return column(sums, 0, width) + (line(sums, half, width) + 1e-6)
 
     def coupling(n, denom):
-        wait_recv(gram.at[n, others], g_recv.at[n])
+        wait_recv(gram.at[n, :, others], g_recv.at[n])
         return gram[n].reshape(width, width) / denom
 
     ident = (
@@ -248,20 +254,22 @@
         == lax.broadcasted_iota(jnp.int32, (width, width), 1)
     ).astype(jnp.float32)
 
-    def rotate(couple, keep, sign_other):
-        other, sign = sign_other
-        scale = 1.0 + jnp.sum(couple * couple, keepdims=True)
-        inv = 1.0 / scale
-        pieces = split(couple)
-        inner = (ident + dot3(pieces, pieces, ROWS_BY_ROWS)) * inv
-        out = (keep + sign * dot3(split(other), pieces, ROWS_BY_ROWS)) * jnp.sqrt(inv)
+    def rotate(items):
+        inners, outs = [], []
+        for couple, keep, other, sign in items:
+            pieces = split(couple)
+            scale = 1.0 + jnp.sum(couple * couple, keepdims=True)
+            inv = 1.0 / scale
+            inners.append((ident + dot3(pieces, pieces, ROWS_BY_ROWS)) * inv)
+            mixed = keep + sign * dot3(split(other), pieces, ROWS_BY_ROWS)
+            outs.append(mixed * jnp.sqrt(inv))
         for step in range(NS_STEPS):
-            factor = 1.5 * ident - 0.5 * inner
-            fs = split(factor)
-            out = dot3(split(out), fs)
-            if step + 1 < NS_STEPS:
-                inner = dot3(split(inner), split(dot3(fs, fs)))
-        return out
+            factors = [split(1.5 * ident - 0.5 * inner) for inner in inners]
+            if step + 1 == NS_STEPS:
+                return [dot3(split(out), fs) for out, fs in zip(outs, factors)]
+            inners = [dot3(split(inner), fs) for inner, fs in zip(inners, factors)]
+            outs = [dot3(split(out), fs) for out, fs in zip(outs, factors)]
+            inners = [dot3(split(inner), fs) for inner, fs in zip(inners, factors)]
 
     for side in range(2):
         wait_recv(recv_f.at[side, peers], f_recv.at[side])
@@ -272,31 +280,30 @@
     for side in range(2):
         couple = coupling(side, denoms[side])
         both = recv_f[side].reshape(group, 2 * width)
-        blocks.append(rotate(couple, both[:, :width], (both[:, width:], signs[side])))
+        blocks += rotate([(couple, both[:, :width], both[:, width:], signs[side])])
 
     reduce_start(2, blocks[0], blocks[1])
     couple = coupling(2, reduce_middle(2))
-    finals = [
-        rotate(couple, blocks[0], (blocks[1], -1.0)),
-        rotate(couple.T, blocks[1], (blocks[0], 1.0)),
-    ]
-    for side in range(2):
-        send_b[:, side] = finals[side].reshape(npair, rows, width)
+    finals = rotate(
+        [(couple, *blocks, -1.0), (couple.T, blocks[1], blocks[0], 1.0)]
+    )
+    for side in range(2):
         sums = jnp.sum(finals[side] * finals[side], axis=0, keepdims=True)
         for i in range(half):
             spart[side * half + i : side * half + i + 1, :] = sums[
                 :, i * LANE : (i + 1) * LANE
             ]
-    gather_s[r] = spart[...]
     for k in range(1, nrow):
         copy_to(by_rank[k], spart, gather_s.at[r], s_send, s_recv).start()
+    gather_s[r] = spart[...]
+    for side in range(2):
+        send_b[:, side] = finals[side].reshape(npair, rows, width)
     mine = pl.ds(2 * p, 2)
-    own = pltpu.make_async_copy(send_b.at[p], recv_b.at[mine], in_sem.at[0])
-    own.start()
     for k in range(1, npair):
         copy_to(
             by_slot[k], send_b.at[slots[k]], recv_b.at[mine], b_send, b_recv
         ).start()
+    recv_b[mine] = send_b[p]
 
     wait_recv(gather_s.at[others], s_recv)
     sums = gather_s[0]
@@ -309,47 +316,20 @@
         copy_to(by_slot[k], sfin, recv_s.at[mine], v_send, v_recv).start()
     recv_s[mine] = sfin[...]
 
-    own.wait()
     arrived = pl.ds(0, 2 * (npair - 1))
     wait_send(send_f.at[:, peers], f_send)
     wait_send(gather_d.at[:, others], d_send)
-    wait_send(gather_p.at[:, others], p_send)
-    wait_send(gram.at[:, others], g_send)
+    wait_send(gather_p.at[:, :, others], p_send)
+    wait_send(gram.at[:, :, others], g_send)
     wait_send(gather_s.at[others], s_send)
     wait_send(send_b.at[peers], b_send)
     wait_send(recv_s.at[arrived], v_send)
     wait_recv(recv_b.at[arrived], b_recv)
     wait_recv(recv_s.at[arrived], v_recv)
-
-
-def place(plan_ref, blocks_ref, vals_in, out_ref, vals_ref, buffer, in_sem, out_sem):
-    nblocks, rows, width = blocks_ref.shape
-    half = width // LANE
-    batch = 4
-    slots = [locate(plan_ref, j, nblocks) for j in range(nblocks)]
-    loads, stores = [], []
     for j in range(nblocks):
-        columns = pl.ds(j * width, width)
-        loads.append(
-            pltpu.make_async_copy(
-                blocks_ref.at[slots[j]], buffer.at[:, columns], in_sem.at[j]
-            )
-        )
-        loads[-1].start()
-    for j in range(nblocks):
-        vals_ref[j * half : (j + 1) * half, :] = vals_in[slots[j]]
-    for j in range(0, nblocks, batch):
-        columns = pl.ds(j * width, batch * width)
-        for load in loads[j : j + batch]:
-            load.wait()
-        stores.append(
-            pltpu.make_async_copy(
-                buffer.at[:, columns], out_ref.at[:, columns], out_sem.at[j // batch]
-            )
-        )
-        stores[-1].start()
-    for store in stores:
-        store.wait()
+        slot = locate(plan_ref, j, nblocks)
+        out_ref[:, j * width : (j + 1) * width] = recv_b[slot]
+        vals_ref[j * half : (j + 1) * half, :] = recv_s[slot]
 
 
 def solution(mesh):
@@ -361,28 +341,30 @@
         rows, ncols = slab.shape
         nblocks = 2 * npair
         width = ncols // nblocks
-        part_rows = width // nrow
+        part_rows = width // (nrow * CHUNKS)
         half = width // LANE
         f32 = jnp.float32
         dma = pltpu.SemaphoreType.DMA
-        arrived, arrived_vals = pl.pallas_call(
+        out, vals = pl.pallas_call(
             functools.partial(kernel, rows * nrow * npair),
             out_shape=(
-                jax.ShapeDtypeStruct((nblocks, rows, width), f32),
-                jax.ShapeDtypeStruct((nblocks, half, LANE), f32),
+                pltpu.VMEM((rows, ncols), f32),
+                pltpu.VMEM((nblocks * half, LANE), f32),
             ),
             in_specs=[anywhere, anywhere],
-            out_specs=(anywhere, pl.BlockSpec(memory_space=vmem)),
+            out_specs=(pl.BlockSpec(memory_space=vmem), pl.BlockSpec(memory_space=vmem)),
             scratch_shapes=[
+                vmem((nblocks, rows, width), f32),
+                vmem((nblocks, half, LANE), f32),
                 smem(plan.shape, jnp.int32),
                 vmem((nblocks, rows, width), f32),
                 vmem((2, npair - 1, rows, 2 * width), f32),
                 vmem((2, npair, rows, 2 * width), f32),
-                vmem((3, nrow, part_rows, width), f32),
-                vmem((3, nrow, part_rows, width), f32),
+                vmem((3, CHUNKS, nrow, part_rows, width), f32),
+                vmem((3, CHUNKS, nrow, part_rows, width), f32),
                 vmem((3, 2 * half, LANE), f32),
                 vmem((3, nrow, 2 * half, LANE), f32),
-                vmem((3, nrow, part_rows, width), f32),
+                vmem((3, CHUNKS, nrow, part_rows, width), f32),
                 vmem((npair, 2, rows, width), f32),
                 vmem((2 * half, LANE), f32),
                 vmem((nrow, 2 * half, LANE), f32),
@@ -391,7 +373,7 @@
                 dma,
                 dma((2,)),
                 dma,
-                dma((3,)),
+                dma((3, CHUNKS)),
                 dma,
                 dma((3,)),
                 dma,
@@ -404,24 +386,9 @@
                 dma,
             ],
             compiler_params=pltpu.CompilerParams(
-                collective_id=0, has_side_effects=True, vmem_limit_bytes=67043328
+                collective_id=0, has_side_effects=True, vmem_limit_bytes=66000000
             ),
         )(plan, slab)
-        out, vals = pl.pallas_call(
-            place,
-            out_shape=(
-                jax.ShapeDtypeStruct((rows, ncols), f32),
-                jax.ShapeDtypeStruct((nblocks * half, LANE), f32),
-            ),
-            in_specs=[
-                pl.BlockSpec(memory_space=smem),
-                anywhere,
-                pl.BlockSpec(memory_space=vmem),
-            ],
-            out_specs=(anywhere, pl.BlockSpec(memory_space=vmem)),
-            scratch_shapes=[vmem((rows, ncols), f32), dma((nblocks,)), dma((4,))],
-            compiler_params=pltpu.CompilerParams(vmem_limit_bytes=67043328),
-        )(plan, arrived, arrived_vals)
         return out, vals.reshape(ncols)
 
     return jax.shard_map(

time: 71.5 us -> 64.3 us (0.90)
  Pallas kernels: 70.3 us -> 62 us
  local copies, waits for them, and re-layouts: 0 us -> 1.4 us
    pallas_call x1, Pallas kernels: 67.1 us -> 62 us  [on_device(): pl.pallas_call(functools.partial(kernel, rows * nrow * npair), out_shape=...]
    pallas_call x1 -> x0, Pallas kernels: 3.21 us -> none  [on_device(): pl.pallas_call(place, out_shape=(jax.ShapeDtypeStruct((rows, ncols), f32)...]
    unnamed x0 -> x2, local copies, waits for them, and re-layouts: none -> 1.4 us
where the time goes in v3:
time: 64.3 us; the launch traced here: 64 us
  Pallas kernels  62 us (96%)
  local copies, waits for them, and re-layouts  1.4 us (2%)
    pallas_call x1, Pallas kernels, on_device(): pl.pallas_call(functools.partial(kernel, rows * nrow * npair), out_shape=...  62 us
    unnamed x2, local copies, waits for them, and re-layouts  1.4 us

profile of v3, /device:TPU:0, one launch (start us, length us, event | category | flops | bytes accessed | tf_op | source)
XLA Modules:
  0.0 64.0 jit_solution(1357313724478609316)
XLA Ops:
  0.6 62.0 %shard_map.41 = (f32[32,4096]{1,0:T(8,128)S(1)}, f32[32,128]{1,0:T(8,128)S(1)}) custom-call(s32[2,16]{1,0:T(2,128)} %plan_hbm.1, f32[32,4096]{1,0:T(8,128)} %slab_ref.1), custom_call_target="tpu_custom_call" | custom-call | tf_op jit(solution)/shard_map/pallas_call | solution.py:348
  62.6 0.8 %copy.6 = f32[32,4096]{1,0:T(8,128)} copy(f32[32,4096]{1,0:T(8,128)S(1)} %get-tuple-element.6) | data formatting | bytes 1048576
  63.4 0.6 copy.7

commit v4 on v3

--- a/solution.py
+++ b/solution.py
@@ -63,29 +63,16 @@
             "pair": lax.div(y, 2) * 4 + x,
         }
 
-    turn = lax.rem(x + z + 2 * y_hi, 4)
-    y_other = lax.div(lax.rem(y + 3, 4), 2)
+    inner = y_lo != y_hi
 
     def slot_peer(slot):
-        i, b = lax.div(slot, 2), lax.rem(slot, 2)
-        x0 = lax.rem(i - z - 2 * y_hi + 8, 4)
-        y1 = lax.rem(2 * y_other + 2 - b, 4)
-        z1 = lax.rem(i - x - 2 * lax.div(y1, 2) + 8, 4)
-        first = core == 0
-        return device(
-            jnp.where(first, x0, x),
-            jnp.where(first, 2 * y_hi + b, y1),
-            jnp.where(first, z, z1),
-            core,
-        )
-
-    def rank_peer(rank):
-        far, t = lax.div(rank, 8), lax.rem(lax.div(rank, 2), 4)
-        return device(
-            t, y_lo + 2 * far, lax.rem(turn - t - 2 * far + 8, 4), lax.rem(rank, 2)
-        )
-
-    return 2 * turn + y_lo, (y_hi * 4 + x) * 2 + core, slot_peer, rank_peer
+        h, xx = lax.div(slot, 4), lax.rem(slot, 4)
+        return device(xx, jnp.where(inner, 1 + h, 3 * h), z, core)
+
+    def rank_peer(m):
+        return device(x, 2 * y_hi + lax.rem(lax.div(m, 2), 2), lax.div(m, 4), lax.rem(m, 2))
+
+    return p, r, slot_peer, rank_peer
 
 
 def locate(plan_ref, block, nblocks):
@@ -204,8 +191,11 @@
         copy_to(by_rank[1], ref, ref, sem, sem).wait_send()
 
     def reduce_start(n, first, second):
-        part[n] = dot3(split(first.T), split(second)).reshape(part.shape[1:])
+        turned, right = first.T, split(second)
+        band = width // CHUNKS
         for h in range(CHUNKS):
+            left = split(turned[h * band : (h + 1) * band])
+            part[n, h] = dot3(left, right).reshape(part.shape[2:])
             for k in range(1, nrow):
                 copy_to(
                     by_rank[k], part.at[n, h, ranks[k]], gather_p.at[n, h, r], p_send,
@@ -266,7 +256,10 @@
         for step in range(NS_STEPS):
             factors = [split(1.5 * ident - 0.5 * inner) for inner in inners]
             if step + 1 == NS_STEPS:
-                return [dot3(split(out), fs) for out, fs in zip(outs, factors)]
+                return [
+                    functools.partial(dot3, split(out), fs)
+                    for out, fs in zip(outs, factors)
+                ]
             inners = [dot3(split(inner), fs) for inner, fs in zip(inners, factors)]
             outs = [dot3(split(out), fs) for out, fs in zip(outs, factors)]
             inners = [dot3(split(inner), fs) for inner, fs in zip(inners, factors)]
@@ -280,15 +273,23 @@
     for side in range(2):
         couple = coupling(side, denoms[side])
         both = recv_f[side].reshape(group, 2 * width)
-        blocks += rotate([(couple, both[:, :width], both[:, width:], signs[side])])
+        (last,) = rotate([(couple, both[:, :width], both[:, width:], signs[side])])
+        blocks.append(last())
 
     reduce_start(2, blocks[0], blocks[1])
     couple = coupling(2, reduce_middle(2))
-    finals = rotate(
+    lasts = rotate(
         [(couple, *blocks, -1.0), (couple.T, blocks[1], blocks[0], 1.0)]
     )
     for side in range(2):
-        sums = jnp.sum(finals[side] * finals[side], axis=0, keepdims=True)
+        final = lasts[side]()
+        send_b[side] = final.reshape(npair, rows, width)
+        for k in range(1, npair):
+            copy_to(
+                by_slot[k], send_b.at[side, slots[k]], recv_b.at[2 * p + side], b_send,
+                b_recv,
+            ).start()
+        sums = jnp.sum(final * final, axis=0, keepdims=True)
         for i in range(half):
             spart[side * half + i : side * half + i + 1, :] = sums[
                 :, i * LANE : (i + 1) * LANE
@@ -296,14 +297,9 @@
     for k in range(1, nrow):
         copy_to(by_rank[k], spart, gather_s.at[r], s_send, s_recv).start()
     gather_s[r] = spart[...]
-    for side in range(2):
-        send_b[:, side] = finals[side].reshape(npair, rows, width)
     mine = pl.ds(2 * p, 2)
-    for k in range(1, npair):
-        copy_to(
-            by_slot[k], send_b.at[slots[k]], recv_b.at[mine], b_send, b_recv
-        ).start()
-    recv_b[mine] = send_b[p]
+    for side in range(2):
+        recv_b[2 * p + side] = send_b[side, p]
 
     wait_recv(gather_s.at[others], s_recv)
     sums = gather_s[0]
@@ -322,7 +318,7 @@
     wait_send(gather_p.at[:, :, others], p_send)
     wait_send(gram.at[:, :, others], g_send)
     wait_send(gather_s.at[others], s_send)
-    wait_send(send_b.at[peers], b_send)
+    wait_send(send_b.at[:, peers], b_send)
     wait_send(recv_s.at[arrived], v_send)
     wait_recv(recv_b.at[arrived], b_recv)
     wait_recv(recv_s.at[arrived], v_recv)
@@ -365,7 +361,7 @@
                 vmem((3, 2 * half, LANE), f32),
                 vmem((3, nrow, 2 * half, LANE), f32),
                 vmem((3, CHUNKS, nrow, part_rows, width), f32),
-                vmem((npair, 2, rows, width), f32),
+                vmem((2, npair, rows, width), f32),
                 vmem((2 * half, LANE), f32),
                 vmem((nrow, 2 * half, LANE), f32),
                 vmem((2, half, LANE), f32),

time: 64.3 us -> 62.7 us (0.975)
  Pallas kernels: 62 us -> 60.2 us
    pallas_call x1, Pallas kernels: 62 us -> 60.2 us  [on_device(): pl.pallas_call(functools.partial(kernel, rows * nrow * npair), out_shape=...]
where the time goes in v4:
time: 62.7 us; the launch traced here: 62.3 us
  Pallas kernels  60.2 us (96%)
  local copies, waits for them, and re-layouts  1.4 us (2%)
  between operations  0.64 us (1%)
    pallas_call x1, Pallas kernels, on_device(): pl.pallas_call(functools.partial(kernel, rows * nrow * npair), out_shape=...  60.2 us
    unnamed x2, local copies, waits for them, and re-layouts  1.4 us

profile of v4, /device:TPU:0, one launch (start us, length us, event | category | flops | bytes accessed | tf_op | source)
XLA Modules:
  0.0 62.3 jit_solution(10708558245867805582)
XLA Ops:
  0.6 60.2 %shard_map.41 = (f32[32,4096]{1,0:T(8,128)S(1)}, f32[32,128]{1,0:T(8,128)S(1)}) custom-call(s32[2,16]{1,0:T(2,128)} %plan_hbm.1, f32[32,4096]{1,0:T(8,128)} %slab_ref.1), custom_call_target="tpu_custom_call" | custom-call | tf_op jit(solution)/shard_map/pallas_call | solution.py:344
  60.9 0.8 %copy.6 = f32[32,4096]{1,0:T(8,128)} copy(f32[32,4096]{1,0:T(8,128)S(1)} %get-tuple-element.6) | data formatting | bytes 1048576
  61.7 0.6 copy.7

commit v5 on v4

--- a/solution.py
+++ b/solution.py
@@ -203,6 +203,8 @@
                 ).start()
         for h in range(CHUNKS):
             gather_p[n, h, r] = part[n, h, r]
+
+    def squares_start(n, first, second):
         sums = jnp.concatenate(
             [
                 jnp.sum(first * first, axis=0, keepdims=True),
@@ -229,30 +231,47 @@
                 copy_to(
                     by_rank[k], gram.at[n, h, r], gram.at[n, h, r], g_send, g_recv.at[n]
                 ).start()
+
+    def denominator(n):
         wait_recv(gather_d.at[n, others], d_recv.at[n])
         sums = gather_d[n, 0]
         for j in range(1, nrow):
             sums = sums + gather_d[n, j]
         return column(sums, 0, width) + (line(sums, half, width) + 1e-6)
 
-    def coupling(n, denom):
+    def reduced(n):
         wait_recv(gram.at[n, :, others], g_recv.at[n])
-        return gram[n].reshape(width, width) / denom
+        return gram[n].reshape(width, width)
 
     ident = (
         lax.broadcasted_iota(jnp.int32, (width, width), 0)
         == lax.broadcasted_iota(jnp.int32, (width, width), 1)
     ).astype(jnp.float32)
 
+    def begin(couple, keep, other, sign):
+        pieces = split(couple)
+        scale = 1.0 + jnp.sum(couple * couple, keepdims=True)
+        inv = 1.0 / scale
+        inner = (ident + dot3(pieces, pieces, ROWS_BY_ROWS)) * inv
+        mixed = keep + sign * dot3(split(other), pieces, ROWS_BY_ROWS)
+        return inner, mixed * (0.5 * jnp.sqrt(inv))
+
+    def factors_of(inner):
+        product = None
+        for step in range(NS_STEPS):
+            factor = 1.5 * ident - 0.5 * inner
+            fs = split(factor)
+            product = 2.0 * factor if step == 0 else dot3(split(product), fs)
+            if step + 1 < NS_STEPS:
+                inner = dot3(split(dot3(split(inner), fs)), fs)
+        return split(product)
+
     def rotate(items):
         inners, outs = [], []
-        for couple, keep, other, sign in items:
-            pieces = split(couple)
-            scale = 1.0 + jnp.sum(couple * couple, keepdims=True)
-            inv = 1.0 / scale
-            inners.append((ident + dot3(pieces, pieces, ROWS_BY_ROWS)) * inv)
-            mixed = keep + sign * dot3(split(other), pieces, ROWS_BY_ROWS)
-            outs.append(mixed * jnp.sqrt(inv))
+        for item in items:
+            inner, out = begin(*item)
+            inners.append(inner)
+            outs.append(2.0 * out)
         for step in range(NS_STEPS):
             factors = [split(1.5 * ident - 0.5 * inner) for inner in inners]
             if step + 1 == NS_STEPS:
@@ -268,16 +287,27 @@
         wait_recv(recv_f.at[side, peers], f_recv.at[side])
         both = recv_f[side].reshape(group, 2 * width)
         reduce_start(side, both[:, :width], both[:, width:])
-    denoms = [reduce_middle(side) for side in range(2)]
-    blocks = []
-    for side in range(2):
-        couple = coupling(side, denoms[side])
+        squares_start(side, both[:, :width], both[:, width:])
+    denoms = []
+    for side in range(2):
+        reduce_middle(side)
+        denoms.append(denominator(side))
+    mixes, turns = [], []
+    for side in range(2):
+        couple = reduced(side) / denoms[side]
         both = recv_f[side].reshape(group, 2 * width)
-        (last,) = rotate([(couple, both[:, :width], both[:, width:], signs[side])])
-        blocks.append(last())
-
-    reduce_start(2, blocks[0], blocks[1])
-    couple = coupling(2, reduce_middle(2))
+        inner, mixed = begin(couple, both[:, :width], both[:, width:], signs[side])
+        mixes.append(mixed)
+        if side == 1:
+            reduce_start(2, *mixes)
+        turns.append(factors_of(inner))
+
+    blocks = [dot3(split(mixed), turn) for mixed, turn in zip(mixes, turns)]
+    squares_start(2, *blocks)
+    reduce_middle(2)
+    denom = denominator(2)
+    middle = dot3(split(reduced(2)), turns[1])
+    couple = dot3(turns[0], split(middle)) / denom
     lasts = rotate(
         [(couple, *blocks, -1.0), (couple.T, blocks[1], blocks[0], 1.0)]
     )

time: 62.7 us -> 61.2 us (0.976)
  Pallas kernels: 60.2 us -> 58.6 us
    pallas_call x1, Pallas kernels: 60.2 us -> 58.6 us  [on_device(): pl.pallas_call(functools.partial(kernel, rows * nrow * npair), out_shape=...]
where the time goes in v5:
time: 61.2 us; the launch traced here: 60.7 us
  Pallas kernels  58.6 us (96%)
  local copies, waits for them, and re-layouts  1.4 us (2%)
  between operations  0.64 us (1%)
    pallas_call x1, Pallas kernels, on_device(): pl.pallas_call(functools.partial(kernel, rows * nrow * npair), out_shape=...  58.6 us
    unnamed x2, local copies, waits for them, and re-layouts  1.4 us

profile of v5, /device:TPU:0, one launch (start us, length us, event | category | flops | bytes accessed | tf_op | source)
XLA Modules:
  0.0 60.7 jit_solution(317192841930354526)
XLA Ops:
  0.6 58.6 %shard_map.41 = (f32[32,4096]{1,0:T(8,128)S(1)}, f32[32,128]{1,0:T(8,128)S(1)}) custom-call(s32[2,16]{1,0:T(2,128)} %plan_hbm.1, f32[32,4096]{1,0:T(8,128)} %slab_ref.1), custom_call_target="tpu_custom_call" | custom-call | tf_op jit(solution)/shard_map/pallas_call | solution.py:374
  59.3 0.8 %copy.6 = f32[32,4096]{1,0:T(8,128)} copy(f32[32,4096]{1,0:T(8,128)S(1)} %get-tuple-element.6) | data formatting | bytes 1048576
  60.1 0.6 copy.7

commit v6 on v5

--- a/solution.py
+++ b/solution.py
@@ -131,6 +131,24 @@
         p, r, slot_peer, rank_peer = ring_places(row, pair, nrow, npair)
     slots = [lax.rem(p + k, npair) for k in range(npair)]
     ranks = [lax.rem(r + k, nrow) for k in range(nrow)]
+    if (nrow, npair) == (16, 8):
+        far_first = (2, 1, 3, 0)
+        slots = [
+            lax.rem(lax.div(p, 4) + dy, 2) * 4 + lax.rem(p + dx, 4)
+            for dx in far_first
+            for dy in (1, 0)
+            if dx or dy
+        ]
+        slots = [p] + slots
+        ranks = [
+            (lax.rem(lax.div(r, 4) + dz, 4) * 2 + lax.rem(lax.div(r, 2) + dy, 2)) * 2
+            + lax.rem(r + dc, 2)
+            for dz in far_first
+            for dy in (1, 0)
+            for dc in (1, 0)
+            if dz or dy or dc
+        ]
+        ranks = [r] + ranks
     by_slot = [None] + [slot_peer(slot) for slot in slots[1:]]
     by_rank = [None] + [rank_peer(rank) for rank in ranks[1:]]
     others, peers = pl.ds(0, nrow - 1), pl.ds(0, npair - 1)
@@ -283,15 +301,20 @@
             outs = [dot3(split(out), fs) for out, fs in zip(outs, factors)]
             inners = [dot3(split(inner), fs) for inner, fs in zip(inners, factors)]
 
-    for side in range(2):
-        wait_recv(recv_f.at[side, peers], f_recv.at[side])
-        both = recv_f[side].reshape(group, 2 * width)
-        reduce_start(side, both[:, :width], both[:, width:])
-        squares_start(side, both[:, :width], both[:, width:])
-    denoms = []
-    for side in range(2):
-        reduce_middle(side)
-        denoms.append(denominator(side))
+    wait_recv(recv_f.at[0, peers], f_recv.at[0])
+    both = recv_f[0].reshape(group, 2 * width)
+    reduce_start(0, both[:, :width], both[:, width:])
+    both = recv_f[0].reshape(group, 2 * width)
+    squares_start(0, both[:, :width], both[:, width:])
+    wait_recv(recv_f.at[1, peers], f_recv.at[1])
+    both = recv_f[1].reshape(group, 2 * width)
+    reduce_start(1, both[:, :width], both[:, width:])
+    both = recv_f[1].reshape(group, 2 * width)
+    squares_start(1, both[:, :width], both[:, width:])
+    reduce_middle(0)
+    reduce_middle(1)
+    denoms = [denominator(side) for side in range(2)]
+
     mixes, turns = [], []
     for side in range(2):
         couple = reduced(side) / denoms[side]

time: 61.2 us -> 60 us (0.980)
  Pallas kernels: 58.6 us -> 57.3 us
    pallas_call x1, Pallas kernels: 58.6 us -> 57.3 us  [on_device(): pl.pallas_call(functools.partial(kernel, rows * nrow * npair), out_shape=...]
where the time goes in v6:
time: 60 us; the launch traced here: 59.3 us
  Pallas kernels  57.3 us (96%)
  local copies, waits for them, and re-layouts  1.4 us (2%)
  between operations  0.64 us (1%)
    pallas_call x1, Pallas kernels, on_device(): pl.pallas_call(functools.partial(kernel, rows * nrow * npair), out_shape=...  57.3 us
    unnamed x2, local copies, waits for them, and re-layouts  1.4 us

profile of v6, /device:TPU:0, one launch (start us, length us, event | category | flops | bytes accessed | tf_op | source)
XLA Modules:
  0.0 59.3 jit_solution(13520112454646735885)
XLA Ops:
  0.6 57.3 %shard_map.41 = (f32[32,4096]{1,0:T(8,128)S(1)}, f32[32,128]{1,0:T(8,128)S(1)}) custom-call(s32[2,16]{1,0:T(2,128)} %plan_hbm.1, f32[32,4096]{1,0:T(8,128)} %slab_ref.1), custom_call_target="tpu_custom_call" | custom-call | tf_op jit(solution)/shard_map/pallas_call | solution.py:397
  57.9 0.8 %copy.6 = f32[32,4096]{1,0:T(8,128)} copy(f32[32,4096]{1,0:T(8,128)S(1)} %get-tuple-element.6) | data formatting | bytes 1048576
  58.7 0.6 %copy.7 = f32[4096]{0:T(1024)} copy(f32[4096]{0:T(1024)S(1)} %bitcast.1) | data formatting | bytes 32768

commit v7 on v6

--- a/solution.py
+++ b/solution.py
@@ -132,19 +132,17 @@
     slots = [lax.rem(p + k, npair) for k in range(npair)]
     ranks = [lax.rem(r + k, nrow) for k in range(nrow)]
     if (nrow, npair) == (16, 8):
-        far_first = (2, 1, 3, 0)
+        far_first = ((2, 1), (2, 0), (1, 1), (3, 1), (1, 0), (3, 0), (0, 1), (0, 0))
         slots = [
             lax.rem(lax.div(p, 4) + dy, 2) * 4 + lax.rem(p + dx, 4)
-            for dx in far_first
-            for dy in (1, 0)
+            for dx, dy in far_first
             if dx or dy
         ]
         slots = [p] + slots
         ranks = [
             (lax.rem(lax.div(r, 4) + dz, 4) * 2 + lax.rem(lax.div(r, 2) + dy, 2)) * 2
             + lax.rem(r + dc, 2)
-            for dz in far_first
-            for dy in (1, 0)
+            for dz, dy in far_first
             for dc in (1, 0)
             if dz or dy or dc
         ]

time: 60 us -> 59.8 us (level)
  no operation moved by 1% of the time
where the time goes in v7:
time: 59.8 us; the launch traced here: 58.9 us
  Pallas kernels  56.9 us (95%)
  local copies, waits for them, and re-layouts  1.4 us (2%)
  between operations  0.64 us (1%)
    pallas_call x1, Pallas kernels, on_device(): pl.pallas_call(functools.partial(kernel, rows * nrow * npair), out_shape=...  56.9 us
    unnamed x2, local copies, waits for them, and re-layouts  1.4 us

profile of v7, /device:TPU:0, one launch (start us, length us, event | category | flops | bytes accessed | tf_op | source)
XLA Modules:
  0.0 58.9 jit_solution(14357444302730977137)
XLA Ops:
  0.6 56.9 %shard_map.41 = (f32[32,4096]{1,0:T(8,128)S(1)}, f32[32,128]{1,0:T(8,128)S(1)}) custom-call(s32[2,16]{1,0:T(2,128)} %plan_hbm.1, f32[32,4096]{1,0:T(8,128)} %slab_ref.1), custom_call_target="tpu_custom_call" | custom-call | tf_op jit(solution)/shard_map/pallas_call | solution.py:395
  57.5 0.8 %copy.6 = f32[32,4096]{1,0:T(8,128)} copy(f32[32,4096]{1,0:T(8,128)S(1)} %get-tuple-element.6) | data formatting | bytes 1048576
  58.3 0.6 %copy.7 = f32[4096]{0:T(1024)} copy(f32[4096]{0:T(1024)S(1)} %bitcast.1) | data formatting | bytes 32768

commit v8 on v6

--- a/solution.py
+++ b/solution.py
@@ -8,7 +8,8 @@
 from jax.sharding import PartitionSpec as P
 
 NS_STEPS = 4
-CHUNKS = 2
+BANDS, HALVES = 2, 2
+CHUNKS = BANDS * HALVES
 MESH = pl.DeviceIdType.MESH
 LANE = 128
 ROWS_BY_ROWS = (((1,), (1,)), ((), ()))
@@ -210,15 +211,20 @@
 
     def reduce_start(n, first, second):
         turned, right = first.T, split(second)
-        band = width // CHUNKS
-        for h in range(CHUNKS):
-            left = split(turned[h * band : (h + 1) * band])
-            part[n, h] = dot3(left, right).reshape(part.shape[2:])
-            for k in range(1, nrow):
-                copy_to(
-                    by_rank[k], part.at[n, h, ranks[k]], gather_p.at[n, h, r], p_send,
-                    p_recv.at[n, h],
-                ).start()
+        band, span = width // BANDS, width // HALVES
+        for g in range(BANDS):
+            left = split(turned[g * band : (g + 1) * band])
+            product = dot3(left, right)
+            for c in range(HALVES):
+                h = g * HALVES + c
+                part[n, h] = product[:, c * span : (c + 1) * span].reshape(
+                    part.shape[2:]
+                )
+                for k in range(1, nrow):
+                    copy_to(
+                        by_rank[k], part.at[n, h, ranks[k]], gather_p.at[n, h, r],
+                        p_send, p_recv.at[n, h],
+                    ).start()
         for h in range(CHUNKS):
             gather_p[n, h, r] = part[n, h, r]
 
@@ -259,7 +265,19 @@
 
     def reduced(n):
         wait_recv(gram.at[n, :, others], g_recv.at[n])
-        return gram[n].reshape(width, width)
+        return jnp.concatenate(
+            [
+                jnp.concatenate(
+                    [
+                        gram[n, g * HALVES + c].reshape(width // BANDS, -1)
+                        for c in range(HALVES)
+                    ],
+                    axis=1,
+                )
+                for g in range(BANDS)
+            ],
+            axis=0,
+        )
 
     ident = (
         lax.broadcasted_iota(jnp.int32, (width, width), 0)
@@ -390,7 +408,7 @@
         rows, ncols = slab.shape
         nblocks = 2 * npair
         width = ncols // nblocks
-        part_rows = width // (nrow * CHUNKS)
+        part_rows = width // (nrow * BANDS)
         half = width // LANE
         f32 = jnp.float32
         dma = pltpu.SemaphoreType.DMA
@@ -409,11 +427,11 @@
                 vmem((nblocks, rows, width), f32),
                 vmem((2, npair - 1, rows, 2 * width), f32),
                 vmem((2, npair, rows, 2 * width), f32),
-                vmem((3, CHUNKS, nrow, part_rows, width), f32),
-                vmem((3, CHUNKS, nrow, part_rows, width), f32),
+                vmem((3, CHUNKS, nrow, part_rows, width // HALVES), f32),
+                vmem((3, CHUNKS, nrow, part_rows, width // HALVES), f32),
                 vmem((3, 2 * half, LANE), f32),
                 vmem((3, nrow, 2 * half, LANE), f32),
-                vmem((3, CHUNKS, nrow, part_rows, width), f32),
+                vmem((3, CHUNKS, nrow, part_rows, width // HALVES), f32),
                 vmem((2, npair, rows, width), f32),
                 vmem((2 * half, LANE), f32),
                 vmem((nrow, 2 * half, LANE), f32),

time: 60 us -> 60 us (level)
  no operation moved by 1% of the time
where the time goes in v8:
time: 60 us; the launch traced here: 59.1 us
  Pallas kernels  57 us (95%)
  local copies, waits for them, and re-layouts  1.4 us (2%)
  between operations  0.64 us (1%)
    pallas_call x1, Pallas kernels, on_device(): pl.pallas_call(functools.partial(kernel, rows * nrow * npair), out_shape=...  57 us
    unnamed x2, local copies, waits for them, and re-layouts  1.4 us

profile of v8, /device:TPU:0, one launch (start us, length us, event | category | flops | bytes accessed | tf_op | source)
XLA Modules:
  0.0 59.1 jit_solution(14418566976428271789)
XLA Ops:
  0.6 57.0 %shard_map.41 = (f32[32,4096]{1,0:T(8,128)S(1)}, f32[32,128]{1,0:T(8,128)S(1)}) custom-call(s32[2,16]{1,0:T(2,128)} %plan_hbm.1, f32[32,4096]{1,0:T(8,128)} %slab_ref.1), custom_call_target="tpu_custom_call" | custom-call | tf_op jit(solution)/shard_map/pallas_call | solution.py:415
  57.7 0.8 %copy.6 = f32[32,4096]{1,0:T(8,128)} copy(f32[32,4096]{1,0:T(8,128)S(1)} %get-tuple-element.6) | data formatting | bytes 1048576
  58.5 0.6 %copy.7 = f32[4096]{0:T(1024)} copy(f32[4096]{0:T(1024)S(1)} %bitcast.1) | data formatting | bytes 32768
